TPU v7x, 128 devices: a whole 4x4x4 slice. The times are simulated.
128 devices in a mesh: panel: 32 (over z, x, core), slab: 4 (over y).
Axes of the slice: x: 4, y: 4, z: 4, core: 2. Of those that a mesh axis runs over, the one named last changes fastest.
Arguments:
- charges: bfloat16 [1048576], P(('panel', 'slab')), may hold values from -6 to 6
- target: float32 [1048576], P(('panel', 'slab')), may hold values from -6 to 6
- stencil: bfloat16 [16384, 64, 256], P(('panel', 'slab')), may hold values from -0.375 to 0.375
- near_matrix: bfloat16 [16384, 4, 4096], P(('panel', 'slab')), may hold values from -0.375 to 0.375
- green: float32 [4096, 4096], P(None, ('panel', 'slab')), may hold values from 0.5 to 8
- block_dest: int32 [16384, 1], P(('panel', 'slab')), may hold values from 0 to 127; in each aligned block of 128 rows (0 to 127, 128 to 255, ...) at most 2 rows name the same one
- block_tile: int32 [16384], P(('panel', 'slab')), may hold values from 0 to 511
- near_offset: int32 [16384, 4], P(('panel', 'slab')), may hold values from -8 to 8
Outputs:
- potentials: float32 [1048576], P(('panel', 'slab'))
- gradient: float32 [1048576], P(('panel', 'slab'))
Inputs may be any that keep to these rules, and one draw needn't show every extreme that they name: `block_dest`: in the 128 blocks of one device no owner is named more than 2 times; in some device's blocks one owner is named exactly 2 times.
All inputs are finite; a program needn't handle non-finite values.
Results may differ from a plain program's by a relative error of at most 0.0025.
The roundings to bfloat16 on the way count: a program that leaves them out, or rounds other values in their place, can miss the bound.
Values may be sent and summed in bfloat16 or wider, within the bound.
A program may use at most 128 MiB of HBM per device.

v0:
```python
import math
import jax
import jax.numpy as jnp
from jax import lax
from jax.sharding import PartitionSpec as P

GRID = 4096
TILE = 16
REACH = 8
HIGHEST = lax.Precision.HIGHEST


def extended_2(cells, sides, width):
    for axis, dim in sides:
        count = lax.axis_size(axis)
        ends = count - 1
        head = lax.slice_in_dim(cells, 0, width, axis=dim)
        tail = lax.slice_in_dim(cells, cells.shape[dim] - width, cells.shape[dim], axis=dim)
        cells = jnp.concatenate(
            [
                lax.ppermute(tail, axis, [(i, (i + 1) % count) for i in range(ends)]),
                cells,
                lax.ppermute(head, axis, [((i + 1) % count, i) for i in range(ends)]),
            ],
            axis=dim,
        )
    return cells


def tables(size_in, size_out, modulus, direction):
    row_index = lax.broadcasted_iota(jnp.int32, (size_in, size_out), 0)
    col_index = lax.broadcasted_iota(jnp.int32, (size_in, size_out), 1)
    phase_angle = (
        direction * 2.0 * math.pi / modulus * (row_index * col_index % modulus).astype(jnp.float32)
    )
    return (jnp.cos(phase_angle), jnp.sin(phase_angle))


def rotate(stacked, formula, cosine, sine):
    with_cos = jnp.einsum(formula, stacked, cosine, precision=HIGHEST)
    with_sin = jnp.einsum(formula, stacked, sine, precision=HIGHEST)
    return jnp.stack([with_cos[0] - with_sin[1], with_sin[0] + with_cos[1]])


def twiddle(stacked, cosine, sine):
    return jnp.stack(
        [stacked[0] * cosine - stacked[1] * sine, stacked[0] * sine + stacked[1] * cosine]
    )


def convolve(grid_cells, green_local, devices, regroup):
    row_count = grid_cells.shape[0]
    width = GRID // devices
    shaped = grid_cells.reshape(row_count, width, devices)
    inner_cos, inner_sin = tables(width, width, width, -1.0)
    outer_cos, outer_sin = tables(devices, devices, devices, -1.0)
    local_cos, local_sin = tables(row_count, row_count, row_count, -1.0)
    twist_cos, twist_sin = tables(width, devices, GRID, -1.0)
    spin_cos, spin_sin = tables(row_count, devices, GRID, -1.0)
    partial_value = jnp.stack(
        [
            jnp.einsum("rab,ak->rkb", shaped, inner_cos, precision=HIGHEST),
            jnp.einsum("rab,ak->rkb", shaped, inner_sin, precision=HIGHEST),
        ]
    )
    partial_value = twiddle(partial_value, twist_cos[None], twist_sin[None])
    spectrum = rotate(partial_value, "zrab,bk->zrka", outer_cos, outer_sin)
    spectrum = regroup(spectrum)
    spectrum = rotate(spectrum, "zrsc,sk->zrkc", outer_cos, outer_sin)
    spectrum = twiddle(spectrum, spin_cos[:, :, None], spin_sin[:, :, None])
    spectrum = rotate(spectrum, "zrkc,rm->zmkc", local_cos, local_sin)
    spectrum = spectrum * green_local.reshape(row_count, devices, width)[None]
    spectrum = rotate(spectrum, "zmkc,mq->zqkc", local_cos, -local_sin)
    spectrum = twiddle(spectrum, spin_cos[:, :, None], -spin_sin[:, :, None])
    spectrum = rotate(spectrum, "zqkc,ks->zqsc", outer_cos, -outer_sin)
    spectrum = regroup(spectrum)
    spectrum = rotate(spectrum, "zrka,kq->zrqa", outer_cos, -outer_sin)
    spectrum = twiddle(spectrum, twist_cos.T[None], -twist_sin.T[None])
    real_out = jnp.einsum("rqk,kp->rpq", spectrum[0], inner_cos, precision=HIGHEST)
    real_out = real_out + jnp.einsum("rqk,kp->rpq", spectrum[1], inner_sin, precision=HIGHEST)
    return real_out.reshape(row_count, GRID) * (1.0 / (GRID * GRID))


def local(charges, target, stencil, near_matrix, green, block_dest, block_tile, near_offset):
    devices = lax.axis_size(("panel", "slab"))
    blocks = stencil.shape[0]
    block_size = stencil.shape[1]
    cell_count = stencil.shape[2]
    pair_count = near_offset.shape[1]
    capacity = 2 * blocks // devices
    row_count = GRID // devices
    tile_rows = row_count // TILE
    tile_cols = GRID // TILE
    tile_total = tile_rows * tile_cols
    destination = block_dest[:, 0]
    one_hot = (destination[:, None] == jnp.arange(devices, dtype=jnp.int32)[None, :]).astype(
        jnp.int32
    )
    earlier = jnp.cumsum(one_hot, axis=0) - one_hot
    slot_index = destination * capacity + jnp.sum(earlier * one_hot, axis=1)
    tile_ids = (
        jnp.full((devices * capacity,), -1.0, jnp.float32)
        .at[slot_index]
        .set(block_tile.astype(jnp.float32))
    )

    def regroup(stacked):
        return lax.all_to_all(stacked, ("panel", "slab"), split_axis=2, concat_axis=2, tiled=True)

    def far_field(values):
        tile_values = jnp.einsum("bp,bpt->bt", values, stencil, preferred_element_type=jnp.float32)
        outgoing = (
            jnp.zeros((devices * capacity, cell_count), jnp.float32).at[slot_index].set(tile_values)
        )
        arrived, arrived_ids = (
            lax.all_to_all(
                outgoing.reshape(devices, capacity, cell_count),
                ("panel", "slab"),
                split_axis=0,
                concat_axis=0,
                tiled=True,
            ),
            lax.all_to_all(
                tile_ids.reshape(devices, capacity),
                ("panel", "slab"),
                split_axis=0,
                concat_axis=0,
                tiled=True,
            ),
        )
        where_ids = arrived_ids.reshape(-1)
        owned_tile = jnp.where(where_ids < 0.0, tile_total, where_ids.astype(jnp.int32))
        tile_sums = (
            jnp.zeros((tile_total, cell_count), jnp.float32)
            .at[owned_tile]
            .add(arrived.reshape(-1, cell_count), mode="drop")
        )
        grid_cells = (
            tile_sums.reshape(tile_rows, tile_cols, TILE, TILE)
            .transpose(0, 2, 1, 3)
            .reshape(row_count, GRID)
        )
        field = convolve(grid_cells, green, devices, regroup)
        back_tiles = field.reshape(tile_rows, TILE, tile_cols, TILE).transpose(0, 2, 1, 3)
        back_tiles = back_tiles.reshape(tile_total, cell_count).astype(jnp.bfloat16)
        returning = jnp.take(back_tiles, jnp.minimum(owned_tile, tile_total - 1), axis=0)
        returned = lax.all_to_all(
            returning.reshape(devices, capacity, cell_count),
            ("panel", "slab"),
            split_axis=0,
            concat_axis=0,
            tiled=True,
        )
        own_tiles = returned.reshape(devices * capacity, cell_count)[slot_index]
        return jnp.einsum("bpt,bt->bp", stencil, own_tiles, preferred_element_type=jnp.float32)

    couple = near_matrix.reshape(blocks, pair_count, block_size, block_size)
    positions = jnp.arange(blocks, dtype=jnp.int32)[:, None] + REACH + near_offset
    charge_blocks = charges.reshape(blocks, block_size)
    extended = extended_2(charge_blocks, ((("panel", "slab"), 0),), REACH)
    potentials = far_field(charge_blocks) + jnp.einsum(
        "bkps,bks->bp", couple, extended[positions], preferred_element_type=jnp.float32
    )
    residual = (potentials - target.reshape(blocks, block_size)).astype(jnp.bfloat16)
    terms = jnp.einsum("bkps,bp->bks", couple, residual, preferred_element_type=jnp.float32)
    extended = jnp.zeros((blocks + 2 * REACH, block_size), jnp.float32)
    extended = extended.at[positions.reshape(-1)].add(terms.reshape(-1, block_size))
    rims = jnp.concatenate([extended[:REACH], extended[blocks + REACH :]], axis=0)
    neighbour = extended_2(rims, ((("panel", "slab"), 0),), REACH)
    own_part = extended[REACH : blocks + REACH]
    own_part = own_part.at[:REACH].add(neighbour[:REACH])
    gradient = far_field(residual) + own_part.at[blocks - REACH :].add(neighbour[3 * REACH :])
    return (potentials.reshape(-1), gradient.reshape(-1))


def solution(mesh):
    return jax.shard_map(
        local,
        mesh=mesh,
        in_specs=(
            P(("panel", "slab")),
            P(("panel", "slab")),
            P(("panel", "slab"), None, None),
            P(("panel", "slab"), None, None),
            P(None, ("panel", "slab")),
            P(("panel", "slab"), None),
            P(("panel", "slab")),
            P(("panel", "slab"), None),
        ),
        out_specs=(P(("panel", "slab")), P(("panel", "slab"))),
        check_vma=False,
    )
```

profile of v0, /device:TPU:1, one launch (start us, length us, event | category | flops | bytes accessed | tf_op | source)
XLA Modules:
  0.0 347.5 jit_solution(201239427642557490)
XLA Ops:
  5.4 11.5 %all-to-all-start = ((f32[128,1,2]{2,1,0:T(1,128)}), f32[128,1,2]{2,1,0:T(1,128)S(1)}, u32[]{:S(2)}, u32[]{:S(2)}) async-start(f32[128,1,2]{2,1,0:T(1,128)} %bitcast.3), calls=%async_computation | async-start | bytes 131072 | tf_op jit(solution)/shard_map/all_to_all | solution.py:123
  17.7 2.8 fusion.335
  22.6 3.9 %all-to-all-done = f32[128,1,2]{2,1,0:T(1,128)S(1)} async-done(((f32[128,1,2]{2,1,0:T(1,128)}), f32[128,1,2]{2,1,0:T(1,128)S(1)}, u32[]{:S(2)}, u32[]{:S(2)}) %all-to-all-start) | async-done | bytes 1056 | tf_op jit(solution)/shard_map/all_to_all | solution.py:123
  26.5 5.8 %all-to-all-start.1 = ((f32[128,2,256]{2,1,0:T(2,128)}), f32[128,2,256]{2,1,0:T(2,128)S(1)}, u32[]{:S(2)}, u32[]{:S(2)}) async-start(f32[128,2,256]{2,1,0:T(2,128)} %reshape.321), calls=%async_computation.1 | async-start | bytes 524288 | tf_op jit(solution)/shard_map/all_to_all | solution.py:116
  33.0 10.4 %all-to-all-done.1 = f32[128,2,256]{2,1,0:T(2,128)S(1)} async-done(((f32[128,2,256]{2,1,0:T(2,128)}), f32[128,2,256]{2,1,0:T(2,128)S(1)}, u32[]{:S(2)}, u32[]{:S(2)}) %all-to-all-start.1) | async-done | bytes 262176 | tf_op jit(solution)/shard_map/all_to_all | solution.py:116
  43.6 2.3 scatter_custom_fusion.2
  46.4 2.6 copy.58
  49.0 3.2 reshape_reshape.6
  56.5 4.4 %copy.59 = f32[2,32,128,32]{3,1,0,2:T(8,128)} copy(f32[2,32,128,32]{2,3,1,0:T(8,128)S(1)} %pad_maximum_fusion.1) | data formatting | bytes 2097152 | tf_op jit(solution)/shard_map/stack | solution.py:42
  60.9 4.7 %reshape.479 = f32[128,1,2048]{2,1,0:T(1,128)} reshape(f32[128,2,32,32]{3,2,1,0:T(8,128)} %bitcast.280) | data formatting | bytes 2097152
  65.7 4.1 %all-to-all-start.2 = ((f32[128,1,2048]{2,1,0:T(1,128)}), f32[128,1,2048]{2,1,0:T(1,128)S(1)}, u32[]{:S(2)}, u32[]{:S(2)}) async-start(f32[128,1,2048]{2,1,0:T(1,128)} %reshape.479), calls=%async_computation.2 | async-start | bytes 2097152 | tf_op jit(solution)/shard_map/all_to_all | solution.py:108
  69.9 3.3 collective-permute-start
  73.3 4.0 %collective-permute-start.1 = (bf16[8,64]{1,0:T(8,128)(2,1)S(1)}, bf16[8,64]{1,0:T(8,128)(2,1)S(1)}, u32[]{:S(2)}, u32[]{:S(2)}) collective-permute-start(bf16[8,64]{1,0:T(8,128)(2,1)S(1)} %slice.247), channel_id=1, source_target_pairs={{1,0},{2,1},{3,2},{4,3},{5,4},{6,5},{7,6},{8,7},{9,8},{10,9},{11,1... | collective-permute-start | bytes 3080 | tf_op jit(solution)/shard_map/ppermute | solution.py:23
  77.5 11.7 %all-to-all-done.2 = f32[128,1,2048]{2,1,0:T(1,128)S(1)} async-done(((f32[128,1,2048]{2,1,0:T(1,128)}), f32[128,1,2048]{2,1,0:T(1,128)S(1)}, u32[]{:S(2)}, u32[]{:S(2)}) %all-to-all-start.2) | async-done | bytes 1048608 | tf_op jit(solution)/shard_map/all_to_all | solution.py:108
  89.7 3.2 reduce.12
  92.9 2.7 reshape.480
  95.6 3.7 %copy.60 = f32[2,32,128,32]{2,3,1,0:T(8,128)S(1)} copy(f32[2,32,128,32]{3,1,0,2:T(8,128)} %bitcast.281) | data formatting | bytes 2097152 | tf_op jit(solution)/shard_map/all_to_all | solution.py:108
  100.6 1.2 convolution_bitcast_fusion.17
  102.2 1.6 convolution_bitcast_fusion.14
  103.8 1.6 convolution_bitcast_fusion.15
  110.7 1.4 convolution_bitcast_fusion.12
  112.4 4.4 %copy.66 = f32[2,32,128,32]{3,1,0,2:T(8,128)} copy(f32[2,32,128,32]{2,3,1,0:T(8,128)S(1)} %pad_maximum_fusion.4) | data formatting | bytes 2097152 | tf_op jit(solution)/shard_map/stack | solution.py:42
  116.9 4.7 %reshape.481 = f32[128,1,2048]{2,1,0:T(1,128)} reshape(f32[128,2,32,32]{3,2,1,0:T(8,128)} %bitcast.282) | data formatting | bytes 2097152
  121.5 3.9 %all-to-all-start.3 = ((f32[128,1,2048]{2,1,0:T(1,128)}), f32[128,1,2048]{2,1,0:T(1,128)S(1)}, u32[]{:S(2)}, u32[]{:S(2)}) async-start(f32[128,1,2048]{2,1,0:T(1,128)} %reshape.481), calls=%async_computation.3 | async-start | bytes 2097152 | tf_op jit(solution)/shard_map/all_to_all | solution.py:108
  125.8 7.8 %copy.72 = bf16[128,4,4096]{0,2,1:T(8,128)(2,1)} copy(bf16[128,4,4096]{2,1,0:T(4,128)(2,1)} %param.17) | data formatting | bytes 8388608 | tf_op args[3]
  133.6 13.0 %copy.106 = bf16[128,4,64,64]{3,2,1,0:T(8,128)(2,1)} copy(bf16[128,4,64,64]{0,3,2,1:T(8,128)(2,1)} %bitcast.288) | data formatting | bytes 8388608 | tf_op jit(solution)/shard_map/reshape | solution.py:157
  147.1 1.3 gather_fusion.1
  148.4 3.2 reduce.13
  151.6 2.7 reshape.482
  154.3 3.7 %copy.67 = f32[2,32,128,32]{2,3,1,0:T(8,128)S(1)} copy(f32[2,32,128,32]{3,1,0,2:T(8,128)} %bitcast.283) | data formatting | bytes 2097152 | tf_op jit(solution)/shard_map/all_to_all | solution.py:108
  162.0 1.4 convert_element_type.225
  166.5 9.8 %all-to-all-start.4 = ((bf16[128,2,256]{2,1,0:T(2,128)(2,1)}), bf16[128,2,256]{2,1,0:T(2,128)(2,1)S(1)}, u32[]{:S(2)}, u32[]{:S(2)}) async-start(bf16[128,2,256]{2,1,0:T(2,128)(2,1)} %reshape.324), calls=%async_computation.4 | async-start | bytes 262144 | tf_op jit(solution)/shard_map/all_to_all | solution.py:147
  176.4 5.6 %fusion.36 = f32[128,1,64,1]{2,1,3,0:T(1,128)S(1)} fusion(bf16[128,4,64,64]{3,2,1,0:T(8,128)(2,1)} %copy.106, bf16[128,4,64,1]{2,1,0,3:T(4,128)(2,1)S(1)} %bitcast.309), kind=kOutput, calls=%fused_computation.121 | convolution fusion | flops 4194304 | bytes 4292608 | tf_op jit(solution)/shard_map/bkps,bks->bp/dot_general | solution.py:161
  182.0 4.2 %all-to-all-done.4 = bf16[128,2,256]{2,1,0:T(2,128)(2,1)S(1)} async-done(((bf16[128,2,256]{2,1,0:T(2,128)(2,1)}), bf16[128,2,256]{2,1,0:T(2,128)(2,1)S(1)}, u32[]{:S(2)}, u32[]{:S(2)}) %all-to-all-start.4) | async-done | bytes 131104 | tf_op jit(solution)/shard_map/all_to_all | solution.py:147
  187.1 3.5 %fusion.65 = f32[128,1,64]{2,1,0:T(1,128)S(1)} fusion(bf16[128,64,256]{2,1,0:T(8,128)(2,1)} %param.16, bf16[128,256,1]{1,0,2:T(8,128)(2,1)S(1)} %bitcast.314), kind=kOutput, calls=%fused_computation.143 | convolution fusion | flops 4194304 | bytes 4292608 | tf_op jit(solution)/shard_map/bpt,bt->bp/dot_general | solution.py:155
  192.6 16.4 %all_to_all.50 = f32[128,2,256]{2,1,0:T(2,128)S(1)} all-to-all(f32[128,2,256]{2,1,0:T(2,128)S(1)} %reshape.329), channel_id=1, replica_groups=mesh['panel'=32,'slab'=4] {'panel','slab'}, dimensions={0} | all-to-all | bytes 524288 | tf_op jit(solution)/shard_map/all_to_all | solution.py:116
  209.2 2.1 scatter_custom_fusion.4
  211.8 3.0 copy.74
  214.8 3.2 reshape_reshape.7
  222.3 4.4 %copy.75 = f32[2,32,128,32]{3,1,0,2:T(8,128)} copy(f32[2,32,128,32]{2,3,1,0:T(8,128)S(1)} %pad_maximum_fusion.6) | data formatting | bytes 2097152 | tf_op jit(solution)/shard_map/stack | solution.py:42
  226.7 4.7 %reshape.483 = f32[128,1,2048]{2,1,0:T(1,128)} reshape(f32[128,2,32,32]{3,2,1,0:T(8,128)} %bitcast.284) | data formatting | bytes 2097152
  231.4 4.2 %all-to-all-start.6 = ((f32[128,1,2048]{2,1,0:T(1,128)}), f32[128,1,2048]{2,1,0:T(1,128)S(1)}, u32[]{:S(2)}, u32[]{:S(2)}) async-start(f32[128,1,2048]{2,1,0:T(1,128)} %reshape.483), calls=%async_computation.6 | async-start | bytes 2097152 | tf_op jit(solution)/shard_map/all_to_all | solution.py:108
  235.8 19.2 %all-to-all-done.6 = f32[128,1,2048]{2,1,0:T(1,128)S(1)} async-done(((f32[128,1,2048]{2,1,0:T(1,128)}), f32[128,1,2048]{2,1,0:T(1,128)S(1)}, u32[]{:S(2)}, u32[]{:S(2)}) %all-to-all-start.6) | async-done | bytes 1048608 | tf_op jit(solution)/shard_map/all_to_all | solution.py:108
  254.9 3.2 reduce.14
  258.1 2.7 reshape.484
  260.8 3.9 %copy.76 = f32[2,32,128,32]{2,3,1,0:T(8,128)S(1)} copy(f32[2,32,128,32]{3,1,0,2:T(8,128)} %bitcast.285) | data formatting | bytes 2097152 | tf_op jit(solution)/shard_map/all_to_all | solution.py:108
  267.6 1.6 convolution_bitcast_fusion.4
  269.2 1.6 convolution_bitcast_fusion.5
  276.0 1.5 convolution_bitcast_fusion.2
  277.8 4.4 %copy.82 = f32[2,32,128,32]{3,1,0,2:T(8,128)} copy(f32[2,32,128,32]{2,3,1,0:T(8,128)S(1)} %pad_maximum_fusion.9) | data formatting | bytes 2097152 | tf_op jit(solution)/shard_map/stack | solution.py:42
  282.3 4.7 %reshape.485 = f32[128,1,2048]{2,1,0:T(1,128)} reshape(f32[128,2,32,32]{3,2,1,0:T(8,128)} %bitcast.286) | data formatting | bytes 2097152
  287.0 3.9 %all-to-all-start.7 = ((f32[128,1,2048]{2,1,0:T(1,128)}), f32[128,1,2048]{2,1,0:T(1,128)S(1)}, u32[]{:S(2)}, u32[]{:S(2)}) async-start(f32[128,1,2048]{2,1,0:T(1,128)} %reshape.485), calls=%async_computation.7 | async-start | bytes 2097152 | tf_op jit(solution)/shard_map/all_to_all | solution.py:108
  290.9 4.6 %fusion.89 = f32[128,1,4,64]{3,1,2,0:T(1,128)S(1)} fusion(bf16[128,4,64,64]{3,2,1,0:T(8,128)(2,1)} %copy.106, bf16[128,64,1,1]{1,0,2,3:T(8,128)(2,1)S(1)} %bitcast.302), kind=kOutput, calls=%fused_computation.172 | convolution fusion | flops 4194304 | bytes 4341760 | tf_op jit(solution)/shard_map/bkps,bp->bks/dot_general | solution.py:165
  295.5 2.2 scatter_custom_fusion.5
  297.7 3.3 collective-permute-start.2
  301.0 3.5 %collective-permute-start.3 = (f32[8,64]{1,0:T(8,128)S(1)}, f32[8,64]{1,0:T(8,128)S(1)}, u32[]{:S(2)}, u32[]{:S(2)}) collective-permute-start(f32[8,64]{1,0:T(8,128)S(1)} %get-tuple-element.57), channel_id=1, source_target_pairs={{1,0},{2,1},{3,2},{4,3},{5,4},{6,5},{7,6},{8,7},{9,8},{10,9},{11,1... | collective-permute-start | bytes 6152 | tf_op jit(solution)/shard_map/ppermute | solution.py:23
  305.2 5.0 %all-to-all-done.7 = f32[128,1,2048]{2,1,0:T(1,128)S(1)} async-done(((f32[128,1,2048]{2,1,0:T(1,128)}), f32[128,1,2048]{2,1,0:T(1,128)S(1)}, u32[]{:S(2)}, u32[]{:S(2)}) %all-to-all-start.7) | async-done | bytes 1048608 | tf_op jit(solution)/shard_map/all_to_all | solution.py:108
  310.2 3.1 reduce.15
  313.4 3.0 reshape.486
  316.3 3.7 %copy.83 = f32[2,32,128,32]{2,3,1,0:T(8,128)S(1)} copy(f32[2,32,128,32]{3,1,0,2:T(8,128)} %bitcast.287) | data formatting | bytes 2097152 | tf_op jit(solution)/shard_map/all_to_all | solution.py:108
  323.9 1.4 convert_element_type.231
  328.3 3.9 %all-to-all-start.8 = ((bf16[128,2,256]{2,1,0:T(2,128)(2,1)}), bf16[128,2,256]{2,1,0:T(2,128)(2,1)S(1)}, u32[]{:S(2)}, u32[]{:S(2)}) async-start(bf16[128,2,256]{2,1,0:T(2,128)(2,1)} %reshape.332), calls=%async_computation.8 | async-start | bytes 262144 | tf_op jit(solution)/shard_map/all_to_all | solution.py:147
  332.3 9.8 %all-to-all-done.8 = bf16[128,2,256]{2,1,0:T(2,128)(2,1)S(1)} async-done(((bf16[128,2,256]{2,1,0:T(2,128)(2,1)}), bf16[128,2,256]{2,1,0:T(2,128)(2,1)S(1)}, u32[]{:S(2)}, u32[]{:S(2)}) %all-to-all-start.8) | async-done | bytes 131104 | tf_op jit(solution)/shard_map/all_to_all | solution.py:147
  343.0 3.4 fusion.62
  (130 shorter events, 54.1 us)
Async XLA Ops:
  5.4 21.1 %all-to-all-start = ((f32[128,1,2]{2,1,0:T(1,128)}), f32[128,1,2]{2,1,0:T(1,128)S(1)}, u32[]{:S(2)}, u32[]{:S(2)}) async-start(f32[128,1,2]{2,1,0:T(1,128)} %bitcast.3), calls=%async_computation | async-start | bytes 131072 | tf_op jit(solution)/shard_map/all_to_all | solution.py:123
  26.5 16.9 %all-to-all-start.1 = ((f32[128,2,256]{2,1,0:T(2,128)}), f32[128,2,256]{2,1,0:T(2,128)S(1)}, u32[]{:S(2)}, u32[]{:S(2)}) async-start(f32[128,2,256]{2,1,0:T(2,128)} %reshape.321), calls=%async_computation.1 | async-start | bytes 524288 | tf_op jit(solution)/shard_map/all_to_all | solution.py:116
  60.9 8.9 %copy-start.2 = (bf16[8192]{0:T(1024)(128)(2,1)S(1)}, bf16[8192]{0:T(1024)(128)(2,1)}, u32[]{:S(2)}) copy-start(bf16[8192]{0:T(1024)(128)(2,1)} %param.14) | copy-start | bytes 49156
  60.9 16.4 %copy-start.1 = (f32[4096,32]{0,1:T(8,128)S(1)}, f32[4096,32]{0,1:T(8,128)}, u32[]{:S(2)}) copy-start(f32[4096,32]{0,1:T(8,128)} %param.18) | copy-start | bytes 1572868
  65.7 23.5 %all-to-all-start.2 = ((f32[128,1,2048]{2,1,0:T(1,128)}), f32[128,1,2048]{2,1,0:T(1,128)S(1)}, u32[]{:S(2)}, u32[]{:S(2)}) async-start(f32[128,1,2048]{2,1,0:T(1,128)} %reshape.479), calls=%async_computation.2 | async-start | bytes 2097152 | tf_op jit(solution)/shard_map/all_to_all | solution.py:108
  69.9 77.1 %collective-permute-start = (bf16[8,64]{1,0:T(8,128)(2,1)S(1)}, bf16[8,64]{1,0:T(8,128)(2,1)S(1)}, u32[]{:S(2)}, u32[]{:S(2)}) collective-permute-start(bf16[8,64]{1,0:T(8,128)(2,1)S(1)} %slice.245), channel_id=1, source_target_pairs={{0,1},{1,2},{2,3},{3,4},{4,5},{5,6},{6,7},{7,8},{8,9},{9,10},{10,1... | collective-permute-start | bytes 3080 | tf_op jit(solution)/shard_map/ppermute | solution.py:21
  73.3 73.7 %collective-permute-start.1 = (bf16[8,64]{1,0:T(8,128)(2,1)S(1)}, bf16[8,64]{1,0:T(8,128)(2,1)S(1)}, u32[]{:S(2)}, u32[]{:S(2)}) collective-permute-start(bf16[8,64]{1,0:T(8,128)(2,1)S(1)} %slice.247), channel_id=1, source_target_pairs={{1,0},{2,1},{3,2},{4,3},{5,4},{6,5},{7,6},{8,7},{9,8},{10,9},{11,1... | collective-permute-start | bytes 3080 | tf_op jit(solution)/shard_map/ppermute | solution.py:23
  116.9 8.6 %copy-start.4 = (s32[128,4]{0,1:T(4,128)S(1)}, s32[128,4]{0,1:T(4,128)}, u32[]{:S(2)}) copy-start(s32[128,4]{0,1:T(4,128)} %param.21) | copy-start | bytes 6148
  121.5 26.9 %all-to-all-start.3 = ((f32[128,1,2048]{2,1,0:T(1,128)}), f32[128,1,2048]{2,1,0:T(1,128)S(1)}, u32[]{:S(2)}, u32[]{:S(2)}) async-start(f32[128,1,2048]{2,1,0:T(1,128)} %reshape.481), calls=%async_computation.3 | async-start | bytes 2097152 | tf_op jit(solution)/shard_map/all_to_all | solution.py:108
  133.6 13.0 %copy-start.3 = (f32[8192]{0:T(1024)S(1)}, f32[8192]{0:T(1024)}, u32[]{:S(2)}) copy-start(f32[8192]{0:T(1024)} %param.15) | copy-start | bytes 98308
  166.5 19.6 %all-to-all-start.4 = ((bf16[128,2,256]{2,1,0:T(2,128)(2,1)}), bf16[128,2,256]{2,1,0:T(2,128)(2,1)S(1)}, u32[]{:S(2)}, u32[]{:S(2)}) async-start(bf16[128,2,256]{2,1,0:T(2,128)(2,1)} %reshape.324), calls=%async_computation.4 | async-start | bytes 262144 | tf_op jit(solution)/shard_map/all_to_all | solution.py:147
  187.1 3.6 %copy-start = (bf16[128,64,256]{2,1,0:T(8,128)(2,1)S(1)}, bf16[128,64,256]{2,1,0:T(8,128)(2,1)}, u32[]{:S(2)}) copy-start(bf16[128,64,256]{2,1,0:T(8,128)(2,1)} %param.16) | copy-start | bytes 12582916
  231.4 23.6 %all-to-all-start.6 = ((f32[128,1,2048]{2,1,0:T(1,128)}), f32[128,1,2048]{2,1,0:T(1,128)S(1)}, u32[]{:S(2)}, u32[]{:S(2)}) async-start(f32[128,1,2048]{2,1,0:T(1,128)} %reshape.483), calls=%async_computation.6 | async-start | bytes 2097152 | tf_op jit(solution)/shard_map/all_to_all | solution.py:108
  287.0 23.3 %all-to-all-start.7 = ((f32[128,1,2048]{2,1,0:T(1,128)}), f32[128,1,2048]{2,1,0:T(1,128)S(1)}, u32[]{:S(2)}, u32[]{:S(2)}) async-start(f32[128,1,2048]{2,1,0:T(1,128)} %reshape.485), calls=%async_computation.7 | async-start | bytes 2097152 | tf_op jit(solution)/shard_map/all_to_all | solution.py:108
  297.7 7.5 %collective-permute-start.2 = (f32[8,64]{1,0:T(8,128)S(1)}, f32[8,64]{1,0:T(8,128)S(1)}, u32[]{:S(2)}, u32[]{:S(2)}) collective-permute-start(f32[8,64]{1,0:T(8,128)S(1)} %get-tuple-element.58), channel_id=1, source_target_pairs={{0,1},{1,2},{2,3},{3,4},{4,5},{5,6},{6,7},{7,8},{8,9},{9,10},{10,1... | collective-permute-start | bytes 6152 | tf_op jit(solution)/shard_map/ppermute | solution.py:21
  301.0 31.2 %collective-permute-start.3 = (f32[8,64]{1,0:T(8,128)S(1)}, f32[8,64]{1,0:T(8,128)S(1)}, u32[]{:S(2)}, u32[]{:S(2)}) collective-permute-start(f32[8,64]{1,0:T(8,128)S(1)} %get-tuple-element.57), channel_id=1, source_target_pairs={{1,0},{2,1},{3,2},{4,3},{5,4},{6,5},{7,6},{8,7},{9,8},{10,9},{11,1... | collective-permute-start | bytes 6152 | tf_op jit(solution)/shard_map/ppermute | solution.py:23
  328.3 13.8 %all-to-all-start.8 = ((bf16[128,2,256]{2,1,0:T(2,128)(2,1)}), bf16[128,2,256]{2,1,0:T(2,128)(2,1)S(1)}, u32[]{:S(2)}, u32[]{:S(2)}) async-start(bf16[128,2,256]{2,1,0:T(2,128)(2,1)} %reshape.332), calls=%async_computation.8 | async-start | bytes 262144 | tf_op jit(solution)/shard_map/all_to_all | solution.py:147
where the time goes:
time: 353 us; the launch traced here: 348 us
  local copies, waits for them, and re-layouts  120 us (34%)
  waiting for transfers between devices  64.2 us (18%)
  starting transfers between devices  61.2 us (17%)
  matrix products  57.3 us (16%)
  other arithmetic  26.2 us (7%)
  blocking collectives  16.4 us (5%)
    unnamed x22, local copies, waits for them, and re-layouts  37.9 us
    all_to_all x4, waiting for transfers between devices, regroup(): lax.all_to_all(stacked, ('panel', 'slab'), split_axis=2, concat_axis=2, t...  35.9 us
    another operation x4, local copies, waits for them, and re-layouts, rotate(): return jnp.stack([with_cos[0] - with_sin[1], with_sin[0] + with_cos[1]])  17.8 us
    all_to_all x1, blocking collectives, far_field(): lax.all_to_all(outgoing.reshape(devices, capacity, cell_count), ('panel',...  16.4 us
    all_to_all x4, starting transfers between devices, regroup(): lax.all_to_all(stacked, ('panel', 'slab'), split_axis=2, concat_axis=2, t...  16.1 us
    dot_general x12, matrix products, rotate(): with_sin = jnp.einsum(formula, stacked, sine, precision=HIGHEST)  15.8 us
    all_to_all x5, local copies, waits for them, and re-layouts, regroup(): lax.all_to_all(stacked, ('panel', 'slab'), split_axis=2, concat_axis=2, t...  15.6 us
    dot_general x12, matrix products, rotate(): with_cos = jnp.einsum(formula, stacked, cosine, precision=HIGHEST)  15.3 us
  transfers between devices with their start and end apart: 12, of which 7 were waited for; matrix products, arithmetic and copies ran while one was open for 27% of the time, Pallas kernels for 0%

commit v1 on v0

--- a/solution.py
+++ b/solution.py
@@ -105,7 +105,15 @@
     )
 
     def regroup(stacked):
-        return lax.all_to_all(stacked, ("panel", "slab"), split_axis=2, concat_axis=2, tiled=True)
+        return jnp.concatenate(
+            lax.all_to_all(
+                jnp.stack(jnp.split(stacked, lax.axis_size(("panel", "slab")), axis=2)),
+                ("panel", "slab"),
+                0,
+                0,
+            ),
+            axis=2,
+        )
 
     def far_field(values):
         tile_values = jnp.einsum("bp,bpt->bt", values, stencil, preferred_element_type=jnp.float32)

time: 353 us -> 1060 us (3.00)
  other arithmetic: 26.2 us -> 413 us
  local copies, waits for them, and re-layouts: 120 us -> 435 us
    unnamed x22 -> x530, local copies, waits for them, and re-layouts: 37.9 us -> 368 us
    split x0 -> x60, other arithmetic: none -> 330 us  [regroup(): jnp.split(stacked, lax.axis_size(('panel', 'slab')), axis=2)]
    another operation x4, other arithmetic: 0.28 us -> 57.5 us  [regroup(): jnp.stack(jnp.split(stacked, lax.axis_size(('panel', 'slab')), axis=2))]
    all_to_all x5 -> x0, local copies, waits for them, and re-layouts: 15.6 us -> none  [regroup(): lax.all_to_all(stacked, ('panel', 'slab'), split_axis=2, concat_axis=2, t...]
    reshape x0 -> x4, local copies, waits for them, and re-layouts: none -> 15.6 us  [regroup(): jnp.concatenate(lax.all_to_all(jnp.stack(jnp.split(stacked, lax.axis_size...]
    another operation x4 -> x5, local copies, waits for them, and re-layouts: 17.8 us -> 2.93 us  [regroup(): jnp.stack(jnp.split(stacked, lax.axis_size(('panel', 'slab')), axis=2))]
  transfers between devices with their start and end apart: 12 -> 12, of which waited for: 7 -> 7; matrix products, arithmetic and copies ran while one was open for 27% -> 26% of each run, Pallas kernels for 0% -> 0%
where the time goes in v1:
time: 1060 us; the launch traced here: 1050 us
  local copies, waits for them, and re-layouts  435 us (41%)
  other arithmetic  413 us (39%)
  waiting for transfers between devices  64.8 us (6%)
  starting transfers between devices  60.6 us (6%)
  matrix products  57.7 us (5%)
  blocking collectives  16.4 us (2%)
    unnamed x530, local copies, waits for them, and re-layouts  368 us
    split x60, other arithmetic, regroup(): jnp.split(stacked, lax.axis_size(('panel', 'slab')), axis=2)  330 us
    another operation x4, other arithmetic, regroup(): jnp.stack(jnp.split(stacked, lax.axis_size(('panel', 'slab')), axis=2))  57.5 us
    all_to_all x4, waiting for transfers between devices, regroup(): lax.all_to_all(jnp.stack(jnp.split(stacked, lax.axis_size(('panel', 'slab...  36.3 us
  transfers between devices with their start and end apart: 12, of which 7 were waited for; matrix products, arithmetic and copies ran while one was open for 26% of the time, Pallas kernels for 0%

profile of v1, /device:TPU:1, one launch (start us, length us, event | category | flops | bytes accessed | tf_op | source)
XLA Modules:
  0.0 1050.1 jit_solution(14573575808549127389)
XLA Ops:
  5.4 11.5 %all-to-all-start = ((f32[128,1,2]{2,1,0:T(1,128)}), f32[128,1,2]{2,1,0:T(1,128)S(1)}, u32[]{:S(2)}, u32[]{:S(2)}) async-start(f32[128,1,2]{2,1,0:T(1,128)} %bitcast.3), calls=%async_computation | async-start | bytes 131072 | tf_op jit(solution)/shard_map/all_to_all | solution.py:131
  33.0 10.4 all-to-all-done.1
  62.0 5.8 fusion.769
  67.8 5.9 fusion.1021
  73.7 5.8 fusion.1019
  79.5 5.8 fusion.1017
  85.3 5.8 fusion.1015
  91.1 6.0 fusion.1013
  97.1 5.8 fusion.1011
  102.8 5.8 fusion.1009
  108.6 5.8 fusion.1007
  114.4 6.2 fusion.1005
  120.6 5.8 fusion.1003
  126.3 5.8 fusion.1001
  132.1 5.9 fusion.999
  217.2 14.4 %reduce.1036 = f32[128,2,32,32]{3,2,1,0:T(8,128)} reduce(f32[128,2,32,1,32]{4,3,2,1,0:T(1,128)} %bitcast.23, f32[]{:T(128)} %broadcast.1147), dimensions={3}, to_apply=%bitcast.23.reduce_sub_computation | reduce | bytes 2097156 | tf_op jit(solution)/shard_map/stack | solution.py:110
  247.6 12.2 %all-to-all-done.2 = f32[128,1,2048]{2,1,0:T(1,128)S(1)} async-done(((f32[128,1,2048]{2,1,0:T(1,128)}), f32[128,1,2048]{2,1,0:T(1,128)S(1)}, u32[]{:S(2)}, u32[]{:S(2)}) %all-to-all-start.2) | async-done | bytes 1048608 | tf_op jit(solution)/shard_map/all_to_all | solution.py:109
  263.0 8.3 reshape.1024
  289.6 5.8 fusion.745
  295.4 5.8 fusion.747
  301.2 5.8 fusion.749
  307.0 5.9 fusion.751
  312.9 5.8 fusion.753
  318.7 5.8 fusion.755
  324.5 5.8 fusion.757
  330.2 6.0 fusion.759
  336.2 5.8 fusion.761
  342.0 5.8 fusion.763
  347.8 5.8 fusion.765
  353.6 6.2 fusion.767
  359.7 5.8 fusion.515
  448.3 14.4 %reduce.1038 = f32[128,2,32,32]{3,2,1,0:T(8,128)} reduce(f32[128,2,32,1,32]{4,3,2,1,0:T(1,128)} %bitcast.42, f32[]{:T(128)} %broadcast.1147), dimensions={3}, to_apply=%bitcast.42.reduce_sub_computation | reduce | bytes 2097156 | tf_op jit(solution)/shard_map/stack | solution.py:110
  471.7 7.9 copy.15855
  479.6 13.0 %copy.15889 = bf16[128,4,64,64]{3,2,1,0:T(8,128)(2,1)} copy(bf16[128,4,64,64]{0,3,2,1:T(8,128)(2,1)} %bitcast.1316) | data formatting | bytes 8388608 | tf_op jit(solution)/shard_map/reshape | solution.py:165
  497.5 8.3 reshape.1026
  518.1 9.8 all-to-all-start.4
  544.1 16.4 %all_to_all.50 = f32[128,2,256]{2,1,0:T(2,128)S(1)} all-to-all(f32[128,2,256]{2,1,0:T(2,128)S(1)} %reshape.357), channel_id=1, replica_groups=mesh['panel'=32,'slab'=4] {'panel','slab'}, dimensions={0} | all-to-all | bytes 524288 | tf_op jit(solution)/shard_map/all_to_all | solution.py:124
  574.9 5.8 fusion.491
  580.7 5.8 fusion.493
  586.5 5.9 fusion.495
  592.4 5.8 fusion.497
  598.2 5.8 fusion.499
  604.0 5.8 fusion.501
  609.8 6.0 fusion.503
  615.7 5.8 fusion.505
  621.5 5.8 fusion.507
  627.3 5.8 fusion.509
  633.1 6.2 fusion.511
  639.2 5.8 fusion.513
  733.8 14.4 %reduce.1040 = f32[128,2,32,32]{3,2,1,0:T(8,128)} reduce(f32[128,2,32,1,32]{4,3,2,1,0:T(1,128)} %bitcast.70, f32[]{:T(128)} %broadcast.1147), dimensions={3}, to_apply=%bitcast.70.reduce_sub_computation | reduce | bytes 2097156 | tf_op jit(solution)/shard_map/stack | solution.py:110
  757.2 19.2 %all-to-all-done.6 = f32[128,1,2048]{2,1,0:T(1,128)S(1)} async-done(((f32[128,1,2048]{2,1,0:T(1,128)}), f32[128,1,2048]{2,1,0:T(1,128)S(1)}, u32[]{:S(2)}, u32[]{:S(2)}) %all-to-all-start.6) | async-done | bytes 1048608 | tf_op jit(solution)/shard_map/all_to_all | solution.py:109
  779.6 8.3 reshape.1028
  806.2 5.8 fusion.237
  823.6 5.9 fusion.243
  829.5 5.8 fusion.245
  835.3 5.8 fusion.247
  846.8 6.0 fusion.251
  852.8 5.8 fusion.253
  858.6 5.8 fusion.255
  864.4 5.8 fusion.257
  870.2 6.2 fusion.259
  964.9 14.4 %reduce.1042 = f32[128,2,32,32]{3,2,1,0:T(8,128)} reduce(f32[128,2,32,1,32]{4,3,2,1,0:T(1,128)} %bitcast.84, f32[]{:T(128)} %broadcast.1147), dimensions={3}, to_apply=%bitcast.84.reduce_sub_computation | reduce | bytes 2097156 | tf_op jit(solution)/shard_map/stack | solution.py:110
  1010.6 8.5 reshape.1030
  1035.0 9.8 all-to-all-done.8
  (698 shorter events, 572.0 us)
Async XLA Ops:
  5.4 21.2 %all-to-all-start = ((f32[128,1,2]{2,1,0:T(1,128)}), f32[128,1,2]{2,1,0:T(1,128)S(1)}, u32[]{:S(2)}, u32[]{:S(2)}) async-start(f32[128,1,2]{2,1,0:T(1,128)} %bitcast.3), calls=%async_computation | async-start | bytes 131072 | tf_op jit(solution)/shard_map/all_to_all | solution.py:131
  26.6 16.8 %all-to-all-start.1 = ((f32[128,2,256]{2,1,0:T(2,128)}), f32[128,2,256]{2,1,0:T(2,128)S(1)}, u32[]{:S(2)}, u32[]{:S(2)}) async-start(f32[128,2,256]{2,1,0:T(2,128)} %reshape.345), calls=%async_computation.1 | async-start | bytes 524288 | tf_op jit(solution)/shard_map/all_to_all | solution.py:124
  231.5 8.9 copy-start.2
  231.5 15.9 %copy-start.1 = (f32[4096,32]{0,1:T(8,128)S(1)}, f32[4096,32]{0,1:T(8,128)}, u32[]{:S(2)}) copy-start(f32[4096,32]{0,1:T(8,128)} %param.18) | copy-start | bytes 1572868
  236.3 23.6 %all-to-all-start.2 = ((f32[128,1,2048]{2,1,0:T(1,128)}), f32[128,1,2048]{2,1,0:T(1,128)S(1)}, u32[]{:S(2)}, u32[]{:S(2)}) async-start(f32[128,1,2048]{2,1,0:T(1,128)} %reshape.1023), calls=%async_computation.2 | async-start | bytes 2097152 | tf_op jit(solution)/shard_map/all_to_all | solution.py:109
  240.5 252.4 %collective-permute-start = (bf16[8,64]{1,0:T(8,128)(2,1)S(1)}, bf16[8,64]{1,0:T(8,128)(2,1)S(1)}, u32[]{:S(2)}, u32[]{:S(2)}) collective-permute-start(bf16[8,64]{1,0:T(8,128)(2,1)S(1)} %slice.245), channel_id=1, source_target_pairs={{0,1},{1,2},{2,3},{3,4},{4,5},{5,6},{6,7},{7,8},{8,9},{9,10},{10,1... | collective-permute-start | bytes 3080 | tf_op jit(solution)/shard_map/ppermute | solution.py:21
  243.9 249.1 %collective-permute-start.1 = (bf16[8,64]{1,0:T(8,128)(2,1)S(1)}, bf16[8,64]{1,0:T(8,128)(2,1)S(1)}, u32[]{:S(2)}, u32[]{:S(2)}) collective-permute-start(bf16[8,64]{1,0:T(8,128)(2,1)S(1)} %slice.247), channel_id=1, source_target_pairs={{1,0},{2,1},{3,2},{4,3},{5,4},{6,5},{7,6},{8,7},{9,8},{10,9},{11,1... | collective-permute-start | bytes 3080 | tf_op jit(solution)/shard_map/ppermute | solution.py:23
  462.6 8.7 copy-start.4
  467.5 26.8 %all-to-all-start.3 = ((f32[128,1,2048]{2,1,0:T(1,128)}), f32[128,1,2048]{2,1,0:T(1,128)S(1)}, u32[]{:S(2)}, u32[]{:S(2)}) async-start(f32[128,1,2048]{2,1,0:T(1,128)} %reshape.1025), calls=%async_computation.3 | async-start | bytes 2097152 | tf_op jit(solution)/shard_map/all_to_all | solution.py:109
  479.6 13.0 %copy-start.3 = (f32[8192]{0:T(1024)S(1)}, f32[8192]{0:T(1024)}, u32[]{:S(2)}) copy-start(f32[8192]{0:T(1024)} %param.15) | copy-start | bytes 98308
  518.1 19.6 %all-to-all-start.4 = ((bf16[128,2,256]{2,1,0:T(2,128)(2,1)}), bf16[128,2,256]{2,1,0:T(2,128)(2,1)S(1)}, u32[]{:S(2)}, u32[]{:S(2)}) async-start(bf16[128,2,256]{2,1,0:T(2,128)(2,1)} %reshape.352), calls=%async_computation.4 | async-start | bytes 262144 | tf_op jit(solution)/shard_map/all_to_all | solution.py:155
  538.6 3.6 copy-start
  752.9 23.5 %all-to-all-start.6 = ((f32[128,1,2048]{2,1,0:T(1,128)}), f32[128,1,2048]{2,1,0:T(1,128)S(1)}, u32[]{:S(2)}, u32[]{:S(2)}) async-start(f32[128,1,2048]{2,1,0:T(1,128)} %reshape.1027), calls=%async_computation.6 | async-start | bytes 2097152 | tf_op jit(solution)/shard_map/all_to_all | solution.py:109
  984.2 23.3 %all-to-all-start.7 = ((f32[128,1,2048]{2,1,0:T(1,128)}), f32[128,1,2048]{2,1,0:T(1,128)S(1)}, u32[]{:S(2)}, u32[]{:S(2)}) async-start(f32[128,1,2048]{2,1,0:T(1,128)} %reshape.1029), calls=%async_computation.7 | async-start | bytes 2097152 | tf_op jit(solution)/shard_map/all_to_all | solution.py:109
  994.9 7.5 collective-permute-start.2
  998.2 36.8 %collective-permute-start.3 = (f32[8,64]{1,0:T(8,128)S(1)}, f32[8,64]{1,0:T(8,128)S(1)}, u32[]{:S(2)}, u32[]{:S(2)}) collective-permute-start(f32[8,64]{1,0:T(8,128)S(1)} %get-tuple-element.569), channel_id=1, source_target_pairs={{1,0},{2,1},{3,2},{4,3},{5,4},{6,5},{7,6},{8,7},{9,8},{10,9},{11,1... | collective-permute-start | bytes 6152 | tf_op jit(solution)/shard_map/ppermute | solution.py:23
  1031.1 13.8 %all-to-all-start.8 = ((bf16[128,2,256]{2,1,0:T(2,128)(2,1)}), bf16[128,2,256]{2,1,0:T(2,128)(2,1)S(1)}, u32[]{:S(2)}, u32[]{:S(2)}) async-start(bf16[128,2,256]{2,1,0:T(2,128)(2,1)} %reshape.364), calls=%async_computation.8 | async-start | bytes 262144 | tf_op jit(solution)/shard_map/all_to_all | solution.py:155
